TPU v7x, 32 devices: a whole 2x2x4 slice. The times are simulated.
32 devices in a mesh: gx: 8 (over z, y), gy: 4 (over x, core).
Axes of the slice: x: 2, y: 2, z: 4, core: 2. Of those that a mesh axis runs over, the one named last changes fastest.
Arguments:
- right_side: float32 [64, 128, 128], P('gy', 'gx'), may hold values from -6 to 9
- diagonal: float32 [64, 128, 128], P('gy', 'gx'), may hold values from 0.02 to 0.5
- horizontal: float32 [64, 128, 128], P('gy', 'gx'), may hold values from 0.1 to 1
- vertical: float32 [128], replicated, may hold values from 0.2 to 2
- precond: float32 [2, 128, 128], replicated, may hold values from -4 to 4
- edge_rows: int32 [2, 64], replicated, may hold values from 0 to 63, as said below
Outputs:
- solution_field: float32 [64, 128, 128], P('gy', 'gx')
- residual: float32 [64, 128, 128], P('gy', 'gx')
- residual_sq: float32 [3], replicated
Inputs may be any that keep to these rules, and one draw needn't show every extreme that they name: Each row of edge_rows lists every number 0 to 63 exactly once.
All inputs are finite; a program needn't handle non-finite values.
Results may differ from a plain program's by a relative error of at most 0.00014.
Values sent between devices are 32-bit elements; how exact they have to be, the bound alone decides.
No kernel may reach another device: no remote copies, remote signals or barrier semaphores. Data moves between devices by JAX's collectives and lax.ppermute only.
A program may use at most 64 MiB of HBM per device.

v0:
```python
import jax
import jax.numpy as jnp
from jax import lax
from jax.sharding import PartitionSpec as P

ITERS = 3


def padded(x, sides, width, wrap):
    for axis, dim in sides:
        devices, length = (lax.axis_size(axis), x.shape[dim])
        up = [(i, (i + 1) % devices) for i in range(devices if wrap else devices - 1)]
        down = [(j, i) for i, j in up]
        last = lax.slice_in_dim(x, length - width, length, axis=dim)
        initial = lax.slice_in_dim(x, 0, width, axis=dim)
        before = lax.ppermute(last, axis, up)
        after = lax.ppermute(initial, axis, down)
        x = jnp.concatenate([before, x, after], axis=dim)
    return x


def local_product(left, right):
    return jnp.sum(left * right)


def on_device(right_side, diagonal, horizontal, vertical, precond, edge_rows):
    rows, cols, levels = right_side.shape
    n_gx = lax.axis_size("gx")
    n_gy = lax.axis_size("gy")
    col_index = lax.axis_index("gx")
    row_index = lax.axis_index("gy")
    total_cells = float(rows * cols * levels * n_gx * n_gy)
    half = n_gx // 2
    panel = (col_index >= half).astype(jnp.int32)
    matrix = lax.dynamic_index_in_dim(precond, panel, 0, keepdims=False)
    east_table = jnp.where(col_index == half - 1, edge_rows[0], edge_rows[1])
    west_table = jnp.where(col_index == half, edge_rows[0], edge_rows[1])
    first_row = row_index * rows
    east_local = lax.dynamic_slice_in_dim(east_table, first_row, rows)
    west_local = lax.dynamic_slice_in_dim(west_table, first_row, rows)
    east_border = (col_index == half - 1) | (col_index == n_gx - 1)
    west_border = (col_index == half) | (col_index == 0)
    solution_field = jnp.zeros_like(right_side)
    residual = right_side
    directions = []
    images = []
    norms = []
    for step in range(ITERS):
        pre = jnp.einsum("yxl,kl->yxk", residual, matrix, precision=lax.Precision.HIGHEST)
        wide = padded(pre, (("gx", 1),), 1, True)
        edges = jnp.stack([wide[:, 0], wide[:, -1]], 0)
        whole = lax.all_gather(edges, "gy", axis=1, tiled=True)
        west_fix = jnp.take(whole[0], west_local, axis=0)
        east_fix = jnp.take(whole[1], east_local, axis=0)
        west = jnp.where(west_border, west_fix, edges[0])
        east = jnp.where(east_border, east_fix, edges[1])
        tall = padded(pre, (("gy", 0),), 1, False)
        flat = jnp.pad(pre, ((0, 0), (0, 0), (1, 1)))
        east_side = jnp.concatenate([pre[:, 1:], east[:, None]], 1)
        west_side = jnp.concatenate([west[:, None], pre[:, :-1]], 1)
        beside = east_side + west_side + tall[2:] + tall[:-2]
        column = flat[:, :, 2:] + flat[:, :, :-2]
        image = diagonal * pre + horizontal * (4.0 * pre - beside) + vertical * (2.0 * pre - column)
        count = len(images)
        terms = [local_product(image, older) for older in images]
        terms = terms + [local_product(residual, older) for older in images]
        terms = terms + [local_product(image, image), local_product(residual, image)]
        if step > 0:
            terms.append(local_product(residual, residual))
        totals = lax.psum(jnp.stack(terms), ("gx", "gy")) / total_cells
        coeffs = totals[:count]
        against = totals[count : 2 * count]
        square = totals[2 * count] - jnp.sum(coeffs * coeffs)
        along = totals[2 * count + 1] - jnp.sum(coeffs * against)
        if step > 0:
            norms.append(totals[2 * count + 2])
        for number in range(count):
            pre = pre - coeffs[number] * directions[number]
            image = image - coeffs[number] * images[number]
        scale = 1.0 / jnp.sqrt(square)
        alpha = along * scale
        direction = pre * scale
        image = image * scale
        solution_field = solution_field + alpha * direction
        residual = residual - alpha * image
        directions.append(direction)
        images.append(image)
    norms.append(lax.psum(local_product(residual, residual), ("gx", "gy")) / total_cells)
    return (solution_field, residual, jnp.stack(norms))


def solution(mesh):
    in_specs = (P("gy", "gx", None), P("gy", "gx", None), P("gy", "gx", None), P(), P(), P())
    out_specs = (P("gy", "gx", None), P("gy", "gx", None), P())
    return jax.shard_map(
        on_device, mesh=mesh, in_specs=in_specs, out_specs=out_specs, check_vma=False
    )
```

profile of v0, /device:TPU:0, one launch (start us, length us, event | category | flops | bytes accessed | tf_op | source)
XLA Modules:
  0.0 243.0 jit_solution(2497374235617542815)
XLA Ops:
  0.7 0.9 copy-done
  1.5 1.2 convolution_bitcast_fusion
  2.7 1.3 collective-permute-start.2
  4.0 3.0 %collective-permute-start.3 = (f32[1,16,128]{2,1,0:T(8,128)S(1)}, f32[1,16,128]{2,1,0:T(8,128)S(1)}, u32[]{:S(2)}, u32[]{:S(2)}) collective-permute-start(f32[1,16,128]{2,1,0:T(8,128)S(1)} %get-tuple-element.48), channel_id=1, source_target_pairs={{0,1},{1,2},{2,3},{4,5},{5,6},{6,7},{8,9},{9,10},{10,11},{12,13},{... | collective-permute-start | bytes 24584 | tf_op jit(solution)/shard_map/ppermute | solution.py:16
  7.1 3.0 %collective-permute-start = (f32[16,1,128]{2,0,1:T(8,128)S(1)}, f32[16,1,128]{2,0,1:T(8,128)S(1)}, u32[]{:S(2)}, u32[]{:S(2)}) collective-permute-start(f32[16,1,128]{2,0,1:T(8,128)S(1)} %bitcast.112), channel_id=1, source_target_pairs={{0,4},{4,8},{8,12},{12,16},{16,20},{20,24},{24,28},{28,0},{1,5},{5... | collective-permute-start | bytes 24584 | tf_op jit(solution)/shard_map/ppermute | solution.py:16
  10.1 3.1 %collective-permute-start.1 = (f32[16,1,128]{2,0,1:T(8,128)S(1)}, f32[16,1,128]{2,0,1:T(8,128)S(1)}, u32[]{:S(2)}, u32[]{:S(2)}) collective-permute-start(f32[16,1,128]{2,0,1:T(8,128)S(1)} %bitcast.111), channel_id=1, source_target_pairs={{4,0},{8,4},{12,8},{16,12},{20,16},{24,20},{28,24},{0,28},{5,1},{9... | collective-permute-start | bytes 24584 | tf_op jit(solution)/shard_map/ppermute | solution.py:17
  13.3 0.7 copy-done.5
  14.0 0.1 compare_and_fusion.1
  14.0 0.1 compare_and_fusion
  14.2 0.7 collective-permute-done
  14.8 5.4 %all_gather.9 = f32[2,64,128]{2,1,0:T(8,128)S(1)} all-gather(f32[2,16,128]{2,1,0:T(8,128)S(1)} %pad_maximum_fusion.6), channel_id=1, replica_groups=mesh['gx'=8,'gy'=4] {'gy'}, dimensions={1}, use_global_device_ids=true | all-gather | bytes 81920 | tf_op jit(solution)/shard_map/all_gather | solution.py:52
  20.2 0.6 gather_fusion
  20.8 0.6 gather_fusion.1
  21.5 0.6 copy-done.4
  22.2 0.7 multiply_reduce_fusion.14
  22.9 1.4 pad_maximum_fusion.9
  24.3 40.2 %psum.28 = f32[2]{0:T(128)S(1)} all-reduce(f32[2]{0:T(128)S(1)} %pad_maximum_fusion.9), channel_id=1, replica_groups=mesh['gx'=8,'gy'=4] {'gx','gy'}, use_global_device_ids=true, to_apply=%region_2.4 | all-reduce | flops 2 | bytes 16 | tf_op jit(solution)/shard_map/psum | solution.py:70
  64.5 0.6 fusion.54
  66.5 0.3 fusion.29
  66.8 2.3 collective-permute-start.4
  69.1 2.5 %collective-permute-start.5 = (f32[16,1,128]{2,0,1:T(8,128)S(1)}, f32[16,1,128]{2,0,1:T(8,128)S(1)}, u32[]{:S(2)}, u32[]{:S(2)}) collective-permute-start(f32[16,1,128]{2,0,1:T(8,128)S(1)} %bitcast.113), channel_id=1, source_target_pairs={{4,0},{8,4},{12,8},{16,12},{20,16},{24,20},{28,24},{0,28},{5,1},{9... | collective-permute-start | bytes 24584 | tf_op jit(solution)/shard_map/ppermute | solution.py:17
  71.6 1.3 collective-permute-start.6
  72.9 3.0 %collective-permute-start.7 = (f32[1,16,128]{2,1,0:T(8,128)S(1)}, f32[1,16,128]{2,1,0:T(8,128)S(1)}, u32[]{:S(2)}, u32[]{:S(2)}) collective-permute-start(f32[1,16,128]{2,1,0:T(8,128)S(1)} %get-tuple-element.42), channel_id=1, source_target_pairs={{0,1},{1,2},{2,3},{4,5},{5,6},{6,7},{8,9},{9,10},{10,11},{12,13},{... | collective-permute-start | bytes 24584 | tf_op jit(solution)/shard_map/ppermute | solution.py:16
  75.9 5.8 %all_gather.10 = f32[2,64,128]{2,1,0:T(8,128)S(1)} all-gather(f32[2,16,128]{2,1,0:T(8,128)S(1)} %pad_maximum_fusion.7), channel_id=1, replica_groups=mesh['gx'=8,'gy'=4] {'gy'}, dimensions={1}, use_global_device_ids=true | all-gather | bytes 81920 | tf_op jit(solution)/shard_map/all_gather | solution.py:52
  81.8 0.6 gather_fusion.2
  82.3 0.6 gather_fusion.3
  83.1 0.8 multiply_reduce_fusion.8
  83.8 3.2 %stack.76 = f32[5]{0:T(128)S(1)} concatenate(f32[1]{0:T(128)} %bitcast.28, f32[1]{0:T(128)} %bitcast.29, f32[1]{0:T(128)} %bitcast.30, f32[1]{0:T(128)} %bitcast.31, f32[1]{0:T(128)} %bitcast.32), dimensions={0} | concatenate | bytes 40 | tf_op jit(solution)/shard_map/stack | solution.py:70
  87.1 37.9 %psum.29 = f32[5]{0:T(128)S(1)} all-reduce(f32[5]{0:T(128)S(1)} %stack.76), channel_id=1, replica_groups=mesh['gx'=8,'gy'=4] {'gx','gy'}, use_global_device_ids=true, to_apply=%region_8.10 | all-reduce | flops 5 | bytes 40 | tf_op jit(solution)/shard_map/psum | solution.py:70
  124.9 0.6 fusion.52
  129.4 0.7 multiply_subtract_fusion.1
  130.1 0.3 fusion.27
  130.4 2.3 collective-permute-start.8
  132.7 2.5 %collective-permute-start.9 = (f32[16,1,128]{2,0,1:T(8,128)S(1)}, f32[16,1,128]{2,0,1:T(8,128)S(1)}, u32[]{:S(2)}, u32[]{:S(2)}) collective-permute-start(f32[16,1,128]{2,0,1:T(8,128)S(1)} %bitcast.114), channel_id=1, source_target_pairs={{4,0},{8,4},{12,8},{16,12},{20,16},{24,20},{28,24},{0,28},{5,1},{9... | collective-permute-start | bytes 24584 | tf_op jit(solution)/shard_map/ppermute | solution.py:17
  135.2 1.3 collective-permute-start.10
  136.5 3.0 %collective-permute-start.11 = (f32[1,16,128]{2,1,0:T(8,128)S(1)}, f32[1,16,128]{2,1,0:T(8,128)S(1)}, u32[]{:S(2)}, u32[]{:S(2)}) collective-permute-start(f32[1,16,128]{2,1,0:T(8,128)S(1)} %get-tuple-element.36), channel_id=1, source_target_pairs={{0,1},{1,2},{2,3},{4,5},{5,6},{6,7},{8,9},{9,10},{10,11},{12,13},{... | collective-permute-start | bytes 24584 | tf_op jit(solution)/shard_map/ppermute | solution.py:16
  139.6 5.8 %all_gather.11 = f32[2,64,128]{2,1,0:T(8,128)S(1)} all-gather(f32[2,16,128]{2,1,0:T(8,128)S(1)} %pad_maximum_fusion.8), channel_id=1, replica_groups=mesh['gx'=8,'gy'=4] {'gy'}, dimensions={1}, use_global_device_ids=true | all-gather | bytes 81920 | tf_op jit(solution)/shard_map/all_gather | solution.py:52
  145.4 0.6 gather_fusion.4
  145.9 0.6 gather_fusion.5
  146.7 0.9 multiply_reduce_fusion.1
  147.5 4.5 %stack.85 = f32[7]{0:T(128)S(1)} concatenate(f32[1]{0:T(128)} %bitcast.46, f32[1]{0:T(128)} %bitcast.47, f32[1]{0:T(128)} %bitcast.48, f32[1]{0:T(128)} %bitcast.49, f32[1]{0:T(128)} %bitcast.50, f32[1]{0:T(128)} %bitcast.51, f32[1]{0:T(128)} %bitcast.52), dimensions={0} | concatenate | bytes 56 | tf_op jit(solution)/shard_map/stack | solution.py:70
  152.0 38.1 %psum.30 = f32[7]{0:T(128)S(1)} all-reduce(f32[7]{0:T(128)S(1)} %stack.85), channel_id=1, replica_groups=mesh['gx'=8,'gy'=4] {'gx','gy'}, use_global_device_ids=true, to_apply=%region_16.18 | all-reduce | flops 7 | bytes 56 | tf_op jit(solution)/shard_map/psum | solution.py:70
  190.1 0.8 multiply_reduce_fusion.16
  190.9 0.7 fusion.53
  194.1 2.6 %multiply_add_fusion = f32[16,16,128]{2,1,0:T(8,128)} fusion(f32[16,16,128]{2,1,0:T(8,128)S(1)} %fusion.27, f32[16,16,128]{2,1,0:T(8,128)S(1)} %fusion.29, f32[16,16,128]{2,1,0:T(8,128)S(1)} %convolution_bitcast_fusion, f32[]{:T(128)S(6)} %sqrt.17, f32[]{:T(128)} %bitcast.56, f32[]{:T(128)} %bitcast.55, f32[]{:T(128)S(6)} %mul.267, f32[]{:T(128)} %bitcast.34, ...), kind=kLoop, calls=%fused_computation.51 | loop fusion | flops 458752 | bytes 524324 | tf_op jit(solution)/shard_map/add | solution.py:84
  196.7 2.5 %multiply_reduce_fusion = (f32[]{:T(128)}, f32[16,16,128]{2,1,0:T(8,128)}) fusion(f32[16,16,128]{2,1,0:T(8,128)S(1)} %get-tuple-element.23, f32[]{:T(128)S(6)} %sqrt.17, f32[16,16,128]{2,1,0:T(8,128)S(1)} %get-tuple-element.24, f32[]{:T(128)} %bitcast.56, f32[16,16,128]{2,1,0:T(8,128)S(1)} %get-tuple-element.22, f32[16,16,128]{2,1,0:T(8,128)S(1)} %get-tuple-element.26, ...), kind=kLoop, calls=%fused_computation.49 | loop fusion | flops 327679 | bytes 655384 | tf_op jit(solution)/shard_map/reduce_sum | solution.py:23
  199.2 41.3 %psum.31 = f32[]{:T(128)} all-reduce(f32[]{:T(128)} %get-tuple-element.20), channel_id=1, replica_groups=mesh['gx'=8,'gy'=4] {'gx','gy'}, use_global_device_ids=true, to_apply=%region_20.22 | all-reduce | flops 1 | bytes 8 | tf_op jit(solution)/shard_map/psum | solution.py:88
  241.2 1.8 pad_maximum_fusion.10
  (48 shorter events, 0.7 us)
Async XLA Ops:
  0.6 0.9 copy-start
  2.7 18.8 %collective-permute-start.2 = (f32[1,16,128]{2,1,0:T(8,128)S(1)}, f32[1,16,128]{2,1,0:T(8,128)S(1)}, u32[]{:S(2)}, u32[]{:S(2)}) collective-permute-start(f32[1,16,128]{2,1,0:T(8,128)S(1)} %get-tuple-element.47), channel_id=1, source_target_pairs={{1,0},{2,1},{3,2},{5,4},{6,5},{7,6},{9,8},{10,9},{11,10},{13,12},{... | collective-permute-start | bytes 24584 | tf_op jit(solution)/shard_map/ppermute | solution.py:17
  4.0 17.5 %collective-permute-start.3 = (f32[1,16,128]{2,1,0:T(8,128)S(1)}, f32[1,16,128]{2,1,0:T(8,128)S(1)}, u32[]{:S(2)}, u32[]{:S(2)}) collective-permute-start(f32[1,16,128]{2,1,0:T(8,128)S(1)} %get-tuple-element.48), channel_id=1, source_target_pairs={{0,1},{1,2},{2,3},{4,5},{5,6},{6,7},{8,9},{9,10},{10,11},{12,13},{... | collective-permute-start | bytes 24584 | tf_op jit(solution)/shard_map/ppermute | solution.py:16
  7.1 7.7 %collective-permute-start = (f32[16,1,128]{2,0,1:T(8,128)S(1)}, f32[16,1,128]{2,0,1:T(8,128)S(1)}, u32[]{:S(2)}, u32[]{:S(2)}) collective-permute-start(f32[16,1,128]{2,0,1:T(8,128)S(1)} %bitcast.112), channel_id=1, source_target_pairs={{0,4},{4,8},{8,12},{12,16},{16,20},{20,24},{24,28},{28,0},{1,5},{5... | collective-permute-start | bytes 24584 | tf_op jit(solution)/shard_map/ppermute | solution.py:16
  10.1 4.7 %collective-permute-start.1 = (f32[16,1,128]{2,0,1:T(8,128)S(1)}, f32[16,1,128]{2,0,1:T(8,128)S(1)}, u32[]{:S(2)}, u32[]{:S(2)}) collective-permute-start(f32[16,1,128]{2,0,1:T(8,128)S(1)} %bitcast.111), channel_id=1, source_target_pairs={{4,0},{8,4},{12,8},{16,12},{20,16},{24,20},{28,24},{0,28},{5,1},{9... | collective-permute-start | bytes 24584 | tf_op jit(solution)/shard_map/ppermute | solution.py:17
  13.3 0.7 copy-start.5
  14.8 6.7 %copy-start.3 = (f32[16,16,128]{2,1,0:T(8,128)S(1)}, f32[16,16,128]{2,1,0:T(8,128)}, u32[]{:S(2)}) copy-start(f32[16,16,128]{2,1,0:T(8,128)} %param.9) | copy-start | bytes 393220
  20.2 1.3 copy-start.2
  20.2 1.3 copy-start.1
  21.5 0.7 copy-start.4
  66.8 9.1 %collective-permute-start.4 = (f32[16,1,128]{2,0,1:T(8,128)S(1)}, f32[16,1,128]{2,0,1:T(8,128)S(1)}, u32[]{:S(2)}, u32[]{:S(2)}) collective-permute-start(f32[16,1,128]{2,0,1:T(8,128)S(1)} %bitcast.115), channel_id=1, source_target_pairs={{0,4},{4,8},{8,12},{12,16},{16,20},{20,24},{24,28},{28,0},{1,5},{5... | collective-permute-start | bytes 24584 | tf_op jit(solution)/shard_map/ppermute | solution.py:16
  69.1 6.8 %collective-permute-start.5 = (f32[16,1,128]{2,0,1:T(8,128)S(1)}, f32[16,1,128]{2,0,1:T(8,128)S(1)}, u32[]{:S(2)}, u32[]{:S(2)}) collective-permute-start(f32[16,1,128]{2,0,1:T(8,128)S(1)} %bitcast.113), channel_id=1, source_target_pairs={{4,0},{8,4},{12,8},{16,12},{20,16},{24,20},{28,24},{0,28},{5,1},{9... | collective-permute-start | bytes 24584 | tf_op jit(solution)/shard_map/ppermute | solution.py:17
  71.6 11.5 %collective-permute-start.6 = (f32[1,16,128]{2,1,0:T(8,128)S(1)}, f32[1,16,128]{2,1,0:T(8,128)S(1)}, u32[]{:S(2)}, u32[]{:S(2)}) collective-permute-start(f32[1,16,128]{2,1,0:T(8,128)S(1)} %get-tuple-element.41), channel_id=1, source_target_pairs={{1,0},{2,1},{3,2},{5,4},{6,5},{7,6},{9,8},{10,9},{11,10},{13,12},{... | collective-permute-start | bytes 24584 | tf_op jit(solution)/shard_map/ppermute | solution.py:17
  72.9 10.2 %collective-permute-start.7 = (f32[1,16,128]{2,1,0:T(8,128)S(1)}, f32[1,16,128]{2,1,0:T(8,128)S(1)}, u32[]{:S(2)}, u32[]{:S(2)}) collective-permute-start(f32[1,16,128]{2,1,0:T(8,128)S(1)} %get-tuple-element.42), channel_id=1, source_target_pairs={{0,1},{1,2},{2,3},{4,5},{5,6},{6,7},{8,9},{9,10},{10,11},{12,13},{... | collective-permute-start | bytes 24584 | tf_op jit(solution)/shard_map/ppermute | solution.py:16
  130.4 9.1 %collective-permute-start.8 = (f32[16,1,128]{2,0,1:T(8,128)S(1)}, f32[16,1,128]{2,0,1:T(8,128)S(1)}, u32[]{:S(2)}, u32[]{:S(2)}) collective-permute-start(f32[16,1,128]{2,0,1:T(8,128)S(1)} %bitcast.116), channel_id=1, source_target_pairs={{0,4},{4,8},{8,12},{12,16},{16,20},{20,24},{24,28},{28,0},{1,5},{5... | collective-permute-start | bytes 24584 | tf_op jit(solution)/shard_map/ppermute | solution.py:16
  132.7 6.8 %collective-permute-start.9 = (f32[16,1,128]{2,0,1:T(8,128)S(1)}, f32[16,1,128]{2,0,1:T(8,128)S(1)}, u32[]{:S(2)}, u32[]{:S(2)}) collective-permute-start(f32[16,1,128]{2,0,1:T(8,128)S(1)} %bitcast.114), channel_id=1, source_target_pairs={{4,0},{8,4},{12,8},{16,12},{20,16},{24,20},{28,24},{0,28},{5,1},{9... | collective-permute-start | bytes 24584 | tf_op jit(solution)/shard_map/ppermute | solution.py:17
  135.2 11.5 %collective-permute-start.10 = (f32[1,16,128]{2,1,0:T(8,128)S(1)}, f32[1,16,128]{2,1,0:T(8,128)S(1)}, u32[]{:S(2)}, u32[]{:S(2)}) collective-permute-start(f32[1,16,128]{2,1,0:T(8,128)S(1)} %get-tuple-element.35), channel_id=1, source_target_pairs={{1,0},{2,1},{3,2},{5,4},{6,5},{7,6},{9,8},{10,9},{11,10},{13,12},{... | collective-permute-start | bytes 24584 | tf_op jit(solution)/shard_map/ppermute | solution.py:17
  136.5 10.2 %collective-permute-start.11 = (f32[1,16,128]{2,1,0:T(8,128)S(1)}, f32[1,16,128]{2,1,0:T(8,128)S(1)}, u32[]{:S(2)}, u32[]{:S(2)}) collective-permute-start(f32[1,16,128]{2,1,0:T(8,128)S(1)} %get-tuple-element.36), channel_id=1, source_target_pairs={{0,1},{1,2},{2,3},{4,5},{5,6},{6,7},{8,9},{9,10},{10,11},{12,13},{... | collective-permute-start | bytes 24584 | tf_op jit(solution)/shard_map/ppermute | solution.py:16
where the time goes:
time: 244 us; the launch traced here: 243 us
  blocking collectives  175 us (72%)
  starting transfers between devices  28.6 us (12%)
  local copies, waits for them, and re-layouts  15.2 us (6%)
  other arithmetic  12.7 us (5%)
  between operations  9.45 us (4%)
    psum x3, blocking collectives, on_device(): totals = lax.psum(jnp.stack(terms), ('gx', 'gy')) / total_cells  116 us
    psum x1, blocking collectives, on_device(): lax.psum(local_product(residual, residual), ('gx', 'gy')) / total_cells  41.3 us
    all_gather x3, blocking collectives, on_device(): whole = lax.all_gather(edges, 'gy', axis=1, tiled=True)  17 us
    ppermute x6, starting transfers between devices, padded(): before = lax.ppermute(last, axis, up)  16.8 us
    ppermute x6, starting transfers between devices, padded(): after = lax.ppermute(initial, axis, down)  11.9 us
    another operation x2, local copies, waits for them, and re-layouts, on_device(): totals = lax.psum(jnp.stack(terms), ('gx', 'gy')) / total_cells  7.69 us
    reduce_sum x4, other arithmetic, local_product(): return jnp.sum(left * right)  4.94 us
  transfers between devices with their start and end apart: 12, of which 1 were waited for; matrix products, arithmetic and copies ran while one was open for 2% of the time, Pallas kernels for 0%

commit v1 on v0

--- a/solution.py
+++ b/solution.py
@@ -67,7 +67,11 @@
         terms = terms + [local_product(image, image), local_product(residual, image)]
         if step > 0:
             terms.append(local_product(residual, residual))
-        totals = lax.psum(jnp.stack(terms), ("gx", "gy")) / total_cells
+
+        def _compute_orders(mine, chip_axis, net_axis):
+            return jax.lax.psum(jax.lax.psum(mine, axis_name=chip_axis), axis_name=net_axis)
+
+        totals = _compute_orders(jnp.stack(terms), "gy", net_axis="gx") / total_cells
         coeffs = totals[:count]
         against = totals[count : 2 * count]
         square = totals[2 * count] - jnp.sum(coeffs * coeffs)

time: 244 us -> 203 us (0.83)
  blocking collectives: 175 us -> 133 us
    psum x3 -> x6, blocking collectives: 116 us -> 80.4 us  [the longest x3 60 us: _compute_orders(): jax.lax.psum(jax.lax.psum(mine, axis_name=chip_axis), axis_name=net_axis)]
    ppermute x6, starting transfers between devices: 16.8 us -> 12.3 us  [padded(): before = lax.ppermute(last, axis, up)]
    ppermute x6, starting transfers between devices: 11.9 us -> 16.3 us  [padded(): after = lax.ppermute(initial, axis, down)]
    psum x1, blocking collectives: 41.3 us -> 37 us  [on_device(): lax.psum(local_product(residual, residual), ('gx', 'gy')) / total_cells]
where the time goes in v1:
time: 203 us; the launch traced here: 202 us
  blocking collectives  133 us (66%)
  starting transfers between devices  28.6 us (14%)
  local copies, waits for them, and re-layouts  15.2 us (7%)
  other arithmetic  12.7 us (6%)
  between operations  9.46 us (5%)
    psum x3, blocking collectives, _compute_orders(): jax.lax.psum(jax.lax.psum(mine, axis_name=chip_axis), axis_name=net_axis)  60 us
    psum x1, blocking collectives, on_device(): lax.psum(local_product(residual, residual), ('gx', 'gy')) / total_cells  37 us
    psum x3, blocking collectives, _compute_orders(): jax.lax.psum(mine, axis_name=chip_axis)  20.4 us
    ppermute x6, starting transfers between devices, padded(): after = lax.ppermute(initial, axis, down)  16.3 us
    all_gather x3, blocking collectives, on_device(): whole = lax.all_gather(edges, 'gy', axis=1, tiled=True)  15.8 us
    ppermute x6, starting transfers between devices, padded(): before = lax.ppermute(last, axis, up)  12.3 us
    another operation x2, local copies, waits for them, and re-layouts, on_device(): jnp.stack(terms)  7.69 us
    reduce_sum x4, other arithmetic, local_product(): return jnp.sum(left * right)  4.94 us
  transfers between devices with their start and end apart: 12, of which 1 were waited for; matrix products, arithmetic and copies ran while one was open for 2% of the time, Pallas kernels for 0%

profile of v1, /device:TPU:0, one launch (start us, length us, event | category | flops | bytes accessed | tf_op | source)
XLA Modules:
  0.0 201.7 jit_solution(12590225492900633149)
XLA Ops:
  0.7 0.9 copy-done
  1.5 1.2 convolution_bitcast_fusion
  2.7 1.3 collective-permute-start.2
  4.0 3.0 %collective-permute-start.3 = (f32[1,16,128]{2,1,0:T(8,128)S(1)}, f32[1,16,128]{2,1,0:T(8,128)S(1)}, u32[]{:S(2)}, u32[]{:S(2)}) collective-permute-start(f32[1,16,128]{2,1,0:T(8,128)S(1)} %get-tuple-element.48), channel_id=1, source_target_pairs={{0,1},{1,2},{2,3},{4,5},{5,6},{6,7},{8,9},{9,10},{10,11},{12,13},{... | collective-permute-start | bytes 24584 | tf_op jit(solution)/shard_map/ppermute | solution.py:16
  7.1 3.0 %collective-permute-start = (f32[16,1,128]{2,0,1:T(8,128)S(1)}, f32[16,1,128]{2,0,1:T(8,128)S(1)}, u32[]{:S(2)}, u32[]{:S(2)}) collective-permute-start(f32[16,1,128]{2,0,1:T(8,128)S(1)} %bitcast.112), channel_id=1, source_target_pairs={{0,4},{4,8},{8,12},{12,16},{16,20},{20,24},{24,28},{28,0},{1,5},{5... | collective-permute-start | bytes 24584 | tf_op jit(solution)/shard_map/ppermute | solution.py:16
  10.1 3.1 %collective-permute-start.1 = (f32[16,1,128]{2,0,1:T(8,128)S(1)}, f32[16,1,128]{2,0,1:T(8,128)S(1)}, u32[]{:S(2)}, u32[]{:S(2)}) collective-permute-start(f32[16,1,128]{2,0,1:T(8,128)S(1)} %bitcast.111), channel_id=1, source_target_pairs={{4,0},{8,4},{12,8},{16,12},{20,16},{24,20},{28,24},{0,28},{5,1},{9... | collective-permute-start | bytes 24584 | tf_op jit(solution)/shard_map/ppermute | solution.py:17
  13.3 0.7 copy-done.5
  14.2 0.7 collective-permute-done
  14.8 5.4 %all_gather.9 = f32[2,64,128]{2,1,0:T(8,128)S(1)} all-gather(f32[2,16,128]{2,1,0:T(8,128)S(1)} %pad_maximum_fusion.6), channel_id=1, replica_groups=mesh['gx'=8,'gy'=4] {'gy'}, dimensions={1}, use_global_device_ids=true | all-gather | bytes 81920 | tf_op jit(solution)/shard_map/all_gather | solution.py:52
  20.2 0.6 gather_fusion
  20.8 0.6 gather_fusion.1
  21.5 0.6 copy-done.4
  22.2 0.7 multiply_reduce_fusion.14
  22.9 1.4 pad_maximum_fusion.9
  24.3 7.2 %psum.49 = f32[2]{0:T(128)S(1)} all-reduce(f32[2]{0:T(128)S(1)} %pad_maximum_fusion.9), channel_id=1, replica_groups=mesh['gx'=8,'gy'=4] {'gy'}, use_global_device_ids=true, to_apply=%region_2.4 | all-reduce | flops 2 | bytes 16 | tf_op jit(solution)/shard_map/psum | solution.py:72
  31.5 21.8 %psum.50 = f32[2]{0:T(128)S(1)} all-reduce(f32[2]{0:T(128)S(1)} %psum.49), channel_id=1, replica_groups=mesh['gx'=8,'gy'=4] {'gx'}, use_global_device_ids=true, to_apply=%region_3.5 | all-reduce | flops 2 | bytes 16 | tf_op jit(solution)/shard_map/psum | solution.py:72
  53.3 0.6 fusion.54
  55.3 0.3 fusion.29
  55.7 4.7 %collective-permute-start.5 = (f32[16,1,128]{2,0,1:T(8,128)S(1)}, f32[16,1,128]{2,0,1:T(8,128)S(1)}, u32[]{:S(2)}, u32[]{:S(2)}) collective-permute-start(f32[16,1,128]{2,0,1:T(8,128)S(1)} %bitcast.113), channel_id=1, source_target_pairs={{4,0},{8,4},{12,8},{16,12},{20,16},{24,20},{28,24},{0,28},{5,1},{9... | collective-permute-start | bytes 24584 | tf_op jit(solution)/shard_map/ppermute | solution.py:17
  60.4 1.3 collective-permute-start.6
  61.7 3.0 %collective-permute-start.7 = (f32[1,16,128]{2,1,0:T(8,128)S(1)}, f32[1,16,128]{2,1,0:T(8,128)S(1)}, u32[]{:S(2)}, u32[]{:S(2)}) collective-permute-start(f32[1,16,128]{2,1,0:T(8,128)S(1)} %get-tuple-element.42), channel_id=1, source_target_pairs={{0,1},{1,2},{2,3},{4,5},{5,6},{6,7},{8,9},{9,10},{10,11},{12,13},{... | collective-permute-start | bytes 24584 | tf_op jit(solution)/shard_map/ppermute | solution.py:16
  64.7 5.2 %all_gather.10 = f32[2,64,128]{2,1,0:T(8,128)S(1)} all-gather(f32[2,16,128]{2,1,0:T(8,128)S(1)} %pad_maximum_fusion.7), channel_id=1, replica_groups=mesh['gx'=8,'gy'=4] {'gy'}, dimensions={1}, use_global_device_ids=true | all-gather | bytes 81920 | tf_op jit(solution)/shard_map/all_gather | solution.py:52
  70.0 0.6 gather_fusion.2
  70.5 0.6 gather_fusion.3
  71.3 0.8 multiply_reduce_fusion.8
  72.1 3.2 %stack.76 = f32[5]{0:T(128)S(1)} concatenate(f32[1]{0:T(128)} %bitcast.28, f32[1]{0:T(128)} %bitcast.29, f32[1]{0:T(128)} %bitcast.30, f32[1]{0:T(128)} %bitcast.31, f32[1]{0:T(128)} %bitcast.32), dimensions={0} | concatenate | bytes 40 | tf_op jit(solution)/shard_map/stack | solution.py:74
  75.3 6.0 %psum.51 = f32[5]{0:T(128)S(1)} all-reduce(f32[5]{0:T(128)S(1)} %stack.76), channel_id=1, replica_groups=mesh['gx'=8,'gy'=4] {'gy'}, use_global_device_ids=true, to_apply=%region_9.11 | all-reduce | flops 5 | bytes 40 | tf_op jit(solution)/shard_map/psum | solution.py:72
  81.3 19.1 %psum.52 = f32[5]{0:T(128)S(1)} all-reduce(f32[5]{0:T(128)S(1)} %psum.51), channel_id=1, replica_groups=mesh['gx'=8,'gy'=4] {'gx'}, use_global_device_ids=true, to_apply=%region_10.12 | all-reduce | flops 5 | bytes 40 | tf_op jit(solution)/shard_map/psum | solution.py:72
  100.4 0.6 fusion.52
  104.9 0.7 multiply_subtract_fusion.1
  105.5 0.3 fusion.27
  105.9 0.1 collective-permute-start.8
  106.0 4.7 %collective-permute-start.9 = (f32[16,1,128]{2,0,1:T(8,128)S(1)}, f32[16,1,128]{2,0,1:T(8,128)S(1)}, u32[]{:S(2)}, u32[]{:S(2)}) collective-permute-start(f32[16,1,128]{2,0,1:T(8,128)S(1)} %bitcast.114), channel_id=1, source_target_pairs={{4,0},{8,4},{12,8},{16,12},{20,16},{24,20},{28,24},{0,28},{5,1},{9... | collective-permute-start | bytes 24584 | tf_op jit(solution)/shard_map/ppermute | solution.py:17
  110.6 1.3 collective-permute-start.10
  111.9 3.0 %collective-permute-start.11 = (f32[1,16,128]{2,1,0:T(8,128)S(1)}, f32[1,16,128]{2,1,0:T(8,128)S(1)}, u32[]{:S(2)}, u32[]{:S(2)}) collective-permute-start(f32[1,16,128]{2,1,0:T(8,128)S(1)} %get-tuple-element.36), channel_id=1, source_target_pairs={{0,1},{1,2},{2,3},{4,5},{5,6},{6,7},{8,9},{9,10},{10,11},{12,13},{... | collective-permute-start | bytes 24584 | tf_op jit(solution)/shard_map/ppermute | solution.py:16
  115.0 5.2 %all_gather.11 = f32[2,64,128]{2,1,0:T(8,128)S(1)} all-gather(f32[2,16,128]{2,1,0:T(8,128)S(1)} %pad_maximum_fusion.8), channel_id=1, replica_groups=mesh['gx'=8,'gy'=4] {'gy'}, dimensions={1}, use_global_device_ids=true | all-gather | bytes 81920 | tf_op jit(solution)/shard_map/all_gather | solution.py:52
  120.3 0.6 gather_fusion.4
  120.8 0.6 gather_fusion.5
  121.5 0.9 multiply_reduce_fusion.1
  122.4 4.5 %stack.85 = f32[7]{0:T(128)S(1)} concatenate(f32[1]{0:T(128)} %bitcast.46, f32[1]{0:T(128)} %bitcast.47, f32[1]{0:T(128)} %bitcast.48, f32[1]{0:T(128)} %bitcast.49, f32[1]{0:T(128)} %bitcast.50, f32[1]{0:T(128)} %bitcast.51, f32[1]{0:T(128)} %bitcast.52), dimensions={0} | concatenate | bytes 56 | tf_op jit(solution)/shard_map/stack | solution.py:74
  126.9 7.2 %psum.53 = f32[7]{0:T(128)S(1)} all-reduce(f32[7]{0:T(128)S(1)} %stack.85), channel_id=1, replica_groups=mesh['gx'=8,'gy'=4] {'gy'}, use_global_device_ids=true, to_apply=%region_18.20 | all-reduce | flops 7 | bytes 56 | tf_op jit(solution)/shard_map/psum | solution.py:72
  134.1 19.1 %psum.54 = f32[7]{0:T(128)S(1)} all-reduce(f32[7]{0:T(128)S(1)} %psum.53), channel_id=1, replica_groups=mesh['gx'=8,'gy'=4] {'gx'}, use_global_device_ids=true, to_apply=%region_19.21 | all-reduce | flops 7 | bytes 56 | tf_op jit(solution)/shard_map/psum | solution.py:72
  153.2 0.8 multiply_reduce_fusion.16
  154.0 0.7 fusion.53
  157.2 2.6 %multiply_add_fusion = f32[16,16,128]{2,1,0:T(8,128)} fusion(f32[16,16,128]{2,1,0:T(8,128)S(1)} %fusion.27, f32[16,16,128]{2,1,0:T(8,128)S(1)} %fusion.29, f32[16,16,128]{2,1,0:T(8,128)S(1)} %convolution_bitcast_fusion, f32[]{:T(128)S(6)} %sqrt.17, f32[]{:T(128)} %bitcast.56, f32[]{:T(128)} %bitcast.55, f32[]{:T(128)S(6)} %mul.267, f32[]{:T(128)} %bitcast.34, ...), kind=kLoop, calls=%fused_computation.51 | loop fusion | flops 458752 | bytes 524324 | tf_op jit(solution)/shard_map/add | solution.py:88
  159.8 2.5 %multiply_reduce_fusion = (f32[]{:T(128)}, f32[16,16,128]{2,1,0:T(8,128)}) fusion(f32[16,16,128]{2,1,0:T(8,128)S(1)} %get-tuple-element.23, f32[]{:T(128)S(6)} %sqrt.17, f32[16,16,128]{2,1,0:T(8,128)S(1)} %get-tuple-element.24, f32[]{:T(128)} %bitcast.56, f32[16,16,128]{2,1,0:T(8,128)S(1)} %get-tuple-element.22, f32[16,16,128]{2,1,0:T(8,128)S(1)} %get-tuple-element.26, ...), kind=kLoop, calls=%fused_computation.49 | loop fusion | flops 327679 | bytes 655384 | tf_op jit(solution)/shard_map/reduce_sum | solution.py:23
  162.3 37.0 %psum.55 = f32[]{:T(128)} all-reduce(f32[]{:T(128)} %get-tuple-element.20), channel_id=1, replica_groups=mesh['gx'=8,'gy'=4] {'gx','gy'}, use_global_device_ids=true, to_apply=%region_23.25 | all-reduce | flops 1 | bytes 8 | tf_op jit(solution)/shard_map/psum | solution.py:92
  200.0 1.8 pad_maximum_fusion.10
  (51 shorter events, 0.9 us)
Async XLA Ops:
  0.6 0.9 copy-start
  2.7 18.8 %collective-permute-start.2 = (f32[1,16,128]{2,1,0:T(8,128)S(1)}, f32[1,16,128]{2,1,0:T(8,128)S(1)}, u32[]{:S(2)}, u32[]{:S(2)}) collective-permute-start(f32[1,16,128]{2,1,0:T(8,128)S(1)} %get-tuple-element.47), channel_id=1, source_target_pairs={{1,0},{2,1},{3,2},{5,4},{6,5},{7,6},{9,8},{10,9},{11,10},{13,12},{... | collective-permute-start | bytes 24584 | tf_op jit(solution)/shard_map/ppermute | solution.py:17
  4.0 17.5 %collective-permute-start.3 = (f32[1,16,128]{2,1,0:T(8,128)S(1)}, f32[1,16,128]{2,1,0:T(8,128)S(1)}, u32[]{:S(2)}, u32[]{:S(2)}) collective-permute-start(f32[1,16,128]{2,1,0:T(8,128)S(1)} %get-tuple-element.48), channel_id=1, source_target_pairs={{0,1},{1,2},{2,3},{4,5},{5,6},{6,7},{8,9},{9,10},{10,11},{12,13},{... | collective-permute-start | bytes 24584 | tf_op jit(solution)/shard_map/ppermute | solution.py:16
  7.1 7.7 %collective-permute-start = (f32[16,1,128]{2,0,1:T(8,128)S(1)}, f32[16,1,128]{2,0,1:T(8,128)S(1)}, u32[]{:S(2)}, u32[]{:S(2)}) collective-permute-start(f32[16,1,128]{2,0,1:T(8,128)S(1)} %bitcast.112), channel_id=1, source_target_pairs={{0,4},{4,8},{8,12},{12,16},{16,20},{20,24},{24,28},{28,0},{1,5},{5... | collective-permute-start | bytes 24584 | tf_op jit(solution)/shard_map/ppermute | solution.py:16
  10.1 4.7 %collective-permute-start.1 = (f32[16,1,128]{2,0,1:T(8,128)S(1)}, f32[16,1,128]{2,0,1:T(8,128)S(1)}, u32[]{:S(2)}, u32[]{:S(2)}) collective-permute-start(f32[16,1,128]{2,0,1:T(8,128)S(1)} %bitcast.111), channel_id=1, source_target_pairs={{4,0},{8,4},{12,8},{16,12},{20,16},{24,20},{28,24},{0,28},{5,1},{9... | collective-permute-start | bytes 24584 | tf_op jit(solution)/shard_map/ppermute | solution.py:17
  13.3 0.7 copy-start.5
  14.8 6.7 %copy-start.3 = (f32[16,16,128]{2,1,0:T(8,128)S(1)}, f32[16,16,128]{2,1,0:T(8,128)}, u32[]{:S(2)}) copy-start(f32[16,16,128]{2,1,0:T(8,128)} %param.9) | copy-start | bytes 393220
  20.2 1.3 copy-start.2
  20.2 1.3 copy-start.1
  21.5 0.7 copy-start.4
  55.6 9.1 %collective-permute-start.4 = (f32[16,1,128]{2,0,1:T(8,128)S(1)}, f32[16,1,128]{2,0,1:T(8,128)S(1)}, u32[]{:S(2)}, u32[]{:S(2)}) collective-permute-start(f32[16,1,128]{2,0,1:T(8,128)S(1)} %bitcast.115), channel_id=1, source_target_pairs={{0,4},{4,8},{8,12},{12,16},{16,20},{20,24},{24,28},{28,0},{1,5},{5... | collective-permute-start | bytes 24584 | tf_op jit(solution)/shard_map/ppermute | solution.py:16
  55.7 9.1 %collective-permute-start.5 = (f32[16,1,128]{2,0,1:T(8,128)S(1)}, f32[16,1,128]{2,0,1:T(8,128)S(1)}, u32[]{:S(2)}, u32[]{:S(2)}) collective-permute-start(f32[16,1,128]{2,0,1:T(8,128)S(1)} %bitcast.113), channel_id=1, source_target_pairs={{4,0},{8,4},{12,8},{16,12},{20,16},{24,20},{28,24},{0,28},{5,1},{9... | collective-permute-start | bytes 24584 | tf_op jit(solution)/shard_map/ppermute | solution.py:17
  60.4 10.9 %collective-permute-start.6 = (f32[1,16,128]{2,1,0:T(8,128)S(1)}, f32[1,16,128]{2,1,0:T(8,128)S(1)}, u32[]{:S(2)}, u32[]{:S(2)}) collective-permute-start(f32[1,16,128]{2,1,0:T(8,128)S(1)} %get-tuple-element.41), channel_id=1, source_target_pairs={{1,0},{2,1},{3,2},{5,4},{6,5},{7,6},{9,8},{10,9},{11,10},{13,12},{... | collective-permute-start | bytes 24584 | tf_op jit(solution)/shard_map/ppermute | solution.py:17
  61.7 9.6 %collective-permute-start.7 = (f32[1,16,128]{2,1,0:T(8,128)S(1)}, f32[1,16,128]{2,1,0:T(8,128)S(1)}, u32[]{:S(2)}, u32[]{:S(2)}) collective-permute-start(f32[1,16,128]{2,1,0:T(8,128)S(1)} %get-tuple-element.42), channel_id=1, source_target_pairs={{0,1},{1,2},{2,3},{4,5},{5,6},{6,7},{8,9},{9,10},{10,11},{12,13},{... | collective-permute-start | bytes 24584 | tf_op jit(solution)/shard_map/ppermute | solution.py:16
  105.9 9.1 %collective-permute-start.8 = (f32[16,1,128]{2,0,1:T(8,128)S(1)}, f32[16,1,128]{2,0,1:T(8,128)S(1)}, u32[]{:S(2)}, u32[]{:S(2)}) collective-permute-start(f32[16,1,128]{2,0,1:T(8,128)S(1)} %bitcast.116), channel_id=1, source_target_pairs={{0,4},{4,8},{8,12},{12,16},{16,20},{20,24},{24,28},{28,0},{1,5},{5... | collective-permute-start | bytes 24584 | tf_op jit(solution)/shard_map/ppermute | solution.py:16
  106.0 9.0 %collective-permute-start.9 = (f32[16,1,128]{2,0,1:T(8,128)S(1)}, f32[16,1,128]{2,0,1:T(8,128)S(1)}, u32[]{:S(2)}, u32[]{:S(2)}) collective-permute-start(f32[16,1,128]{2,0,1:T(8,128)S(1)} %bitcast.114), channel_id=1, source_target_pairs={{4,0},{8,4},{12,8},{16,12},{20,16},{24,20},{28,24},{0,28},{5,1},{9... | collective-permute-start | bytes 24584 | tf_op jit(solution)/shard_map/ppermute | solution.py:17
  110.6 10.9 %collective-permute-start.10 = (f32[1,16,128]{2,1,0:T(8,128)S(1)}, f32[1,16,128]{2,1,0:T(8,128)S(1)}, u32[]{:S(2)}, u32[]{:S(2)}) collective-permute-start(f32[1,16,128]{2,1,0:T(8,128)S(1)} %get-tuple-element.35), channel_id=1, source_target_pairs={{1,0},{2,1},{3,2},{5,4},{6,5},{7,6},{9,8},{10,9},{11,10},{13,12},{... | collective-permute-start | bytes 24584 | tf_op jit(solution)/shard_map/ppermute | solution.py:17
  111.9 9.6 %collective-permute-start.11 = (f32[1,16,128]{2,1,0:T(8,128)S(1)}, f32[1,16,128]{2,1,0:T(8,128)S(1)}, u32[]{:S(2)}, u32[]{:S(2)}) collective-permute-start(f32[1,16,128]{2,1,0:T(8,128)S(1)} %get-tuple-element.36), channel_id=1, source_target_pairs={{0,1},{1,2},{2,3},{4,5},{5,6},{6,7},{8,9},{9,10},{10,11},{12,13},{... | collective-permute-start | bytes 24584 | tf_op jit(solution)/shard_map/ppermute | solution.py:16
